TPU v7x, 32 devices: a whole 2x2x4 slice. The times are simulated.
32 devices in a mesh: mem: 4 (over y, x), lat: 2 (over core), lon: 4 (over z).
Axes of the slice: x: 2, y: 2, z: 4, core: 2. Of those that a mesh axis runs over, the one named last changes fastest.
Arguments:
- control: bfloat16 [4, 48, 48, 2048], P('mem', None, 'lat', 'lon'), may hold values from -6 to 6
- ens_pert: bfloat16 [4, 48, 48, 2048], P('mem', None, 'lat', 'lon'), may hold values from -6 to 6
- vertical_mix: bfloat16 [48, 48], replicated, may hold values from -0.875 to 0.875
- obs_values: bfloat16 [8, 8, 48, 1024], P(('lat', 'lon')), may hold values from -6 to 6
- obs_cells: int32 [8, 8, 1024], P(('lat', 'lon')), may hold values from 0 to 12287
- obs_counts: int32 [8, 8], P(('lat', 'lon')), may hold values from 256 to 1024, as said below
Outputs:
- increment: float32 [48, 48, 2048], P('mem', 'lat', 'lon')
- gradient: float32 [4, 48, 48, 2048], P('mem', None, 'lat', 'lon')
Inputs may be any that keep to these rules, and one draw needn't show every extreme that they name: `obs_counts`: live slots per pair of tiles; for some destination tile every source fills all 1024 slots.
All inputs are finite; a program needn't handle non-finite values.
Results may differ from a plain program's by a relative error of at most 0.0056.
Values may be sent and summed in bfloat16 or wider, within the bound.
A program may use at most 128 MiB of HBM per device.

v0:
```python
import functools
import math

import jax
import jax.numpy as jnp
import numpy as np
from jax import lax
from jax.experimental import pallas as pl
from jax.experimental.pallas import tpu as pltpu
from jax.sharding import PartitionSpec as P

HALF = 24
LANES = 128
MESH = pl.DeviceIdType.MESH
F32 = jnp.float32
BF16 = jnp.bfloat16


def taper_table(distance):
    spread = HALF / 3.0
    total = sum((math.exp(-((offset / spread) ** 2)) for offset in range(-HALF, HALF + 1)))
    values = np.exp(-0.5 * (distance / spread) ** 2) / math.sqrt(total)
    return np.where(np.abs(distance) <= HALF, values, 0.0).astype(np.float32)


def group_of(levels, rows):
    return max(g for g in range(1, levels + 1) if levels % g == 0 and g * rows <= 256)


def constants(levels, rows, cols):
    size = levels * rows
    index = np.arange(size)
    level_of = (index[:, None] // rows == np.arange(levels)[None, :]).astype(np.float32)
    row_of = (index[:, None] % rows == np.arange(rows)[None, :]).astype(np.float32)
    group = group_of(levels, rows)
    eye = np.eye(group, dtype=np.float32)
    r = np.arange(rows)
    delta = (r[:, None] - r[None, :]).astype(np.float64)
    lat_w = np.stack([np.kron(eye, taper_table(delta + s * rows)) for s in (0, 1, -1)])
    c = np.arange(cols)
    band = taper_table((c[:, None] - c[None, :]).astype(np.float64))
    slots = LANES // 32
    pack = np.zeros((2, slots * LANES, LANES), np.float32)
    halo_w = np.zeros((2, slots, LANES, LANES), np.float32)
    i = np.arange(LANES).astype(np.float64)
    for g in range(slots):
        for k in range(HALF):
            pack[0, g * LANES + k, 32 * g + k] = 1.0
            pack[1, g * LANES + LANES - HALF + k, 32 * g + k] = 1.0
            halo_w[0, g, 32 * g + k] = taper_table(k - HALF - i)
            halo_w[1, g, 32 * g + k] = taper_table(LANES + k - i)
    return [jnp.asarray(a, BF16) for a in (level_of, row_of, lat_w, band, pack, halo_w)]


def kernel(
    dims,
    control_h, pert_h, mix, values, cells, counts, level_h, row_h, lat_h, band_h, pack_h, halo_h,
    increment, lat_out, edges,
    control, pert, level_of, row_of, lat_w, band, pack, halo_w,
    live, got_v, got_c, loc_v, loc_c, kron_c, kron_f, lhs, rhs, val32, adjoint, field, own_v, halo,
    smoothed, edge_out, edge_in, inc32, part_out, part_in,
    in_s, s1, s2, r2, loc_s, loc_r, lat_s, lat_r, lon_s, lon_r, rs_s, rs_r,
):
    levels, rows, cols, members, n_lat, n_lon, tiles, cap = dims
    size = levels * rows
    parts = members // n_lat
    half = cap // parts
    away = n_lon - 1
    mem, lat, lon = lax.axis_index("mem"), lax.axis_index("lat"), lax.axis_index("lon")
    tile = lat * n_lon + lon
    slots = LANES // 32
    packed = size // slots
    group = group_of(levels, rows)
    block = group * rows
    chunk = size // 3

    def dot(a, b, dims=(((1,), (0,)), ((), ()))):
        return lax.dot_general(a, b, dims, preferred_element_type=F32)

    nt = (((1,), (1,)), ((), ()))

    inputs = [
        pltpu.make_async_copy(src, dst, in_s.at[i])
        for i, (src, dst) in enumerate((
            (level_h, level_of), (row_h, row_of), (control_h, control), (lat_h, lat_w),
            (pack_h, pack), (band_h, band), (halo_h, halo_w), (pert_h, pert),
        ))
    ]
    for copy in inputs:
        copy.start()

    slot = lax.broadcasted_iota(jnp.int32, (1, half), 1)
    for t in range(tiles):
        for h in range(parts):
            live[t, h] = jnp.where(
                slot + h * half < counts[0, t], cells[t : t + 1, h * half : (h + 1) * half], -1
            )

    barrier = pltpu.get_barrier_semaphore()
    for d in range(1, tiles):
        other = lax.rem(tile + d, tiles)
        pl.semaphore_signal(
            barrier, inc=1, device_id_type=MESH,
            device_id={"lat": other // n_lon, "lon": lax.rem(other, n_lon)},
        )
    for d in range(1, members):
        pl.semaphore_signal(
            barrier, inc=1, device_id={"mem": lax.rem(mem + d, members)}, device_id_type=MESH
        )
    pl.semaphore_wait(barrier, tiles + members - 2)

    piece = lax.rem(mem, parts)
    other_lat = lax.rem(mem // parts - lat + 2 * n_lat, n_lat)

    def values_of(t, h):
        return values.at[t, :, pl.ds(pl.multiple_of(h * half, half), half)]

    def leg_one(o):
        other_lon = lax.rem(lon + o, n_lon)
        t = other_lat * n_lon + other_lon
        return [
            pltpu.make_async_remote_copy(
                src_ref=src, dst_ref=dst.at[mem, o - 1], send_sem=s1.at[o - 1, k],
                recv_sem=r2.at[mem, o - 1, k],
                device_id={"lat": other_lat, "lon": other_lon}, device_id_type=MESH,
            )
            for k, (src, dst) in enumerate(((values_of(t, piece), got_v), (live.at[t, piece], got_c)))
        ]

    def straight(d):
        target = lax.rem(lat + d, n_lat)
        t = target * n_lon + lon
        return [
            pltpu.make_async_remote_copy(
                src_ref=src, dst_ref=dst.at[d, h], send_sem=loc_s.at[d, h, k],
                recv_sem=loc_r.at[d, h, k], device_id={"lat": target}, device_id_type=MESH,
            )
            for h in range(parts)
            for k, (src, dst) in enumerate(((values_of(t, h), loc_v), (live.at[t, h], loc_c)))
        ]

    kept = [
        pltpu.make_async_copy(values_of(tile, h), loc_v.at[0, h], loc_r.at[0, h, 0])
        for h in range(parts)
    ]
    for o in sorted(range(1, n_lon), key=lambda o: -min(o, n_lon - o)):
        for copy in leg_one(o):
            copy.start()
    for d in range(1, n_lat):
        for copy in straight(d):
            copy.start()
    for copy in kept:
        copy.start()
    for h in range(parts):
        loc_c[0, h] = live[tile, h]

    def leg_two(d, p):
        return [
            pltpu.make_async_remote_copy(
                src_ref=buf.at[mem, p], dst_ref=buf.at[mem, p], send_sem=s2.at[d, p, k],
                recv_sem=r2.at[mem, p, k],
                device_id={"mem": lax.rem(mem + d, members)}, device_id_type=MESH,
            )
            for k, buf in enumerate((got_v, got_c))
        ]

    def arrived(owner, p):
        for k, buf in enumerate((got_v, got_c)):
            pltpu.make_async_remote_copy(
                src_ref=buf.at[owner, p], dst_ref=buf.at[owner, p], send_sem=s2.at[0, p, k],
                recv_sem=r2.at[owner, p, k],
                device_id={"mem": lax.rem(mem + 1, members)}, device_id_type=MESH,
            ).wait_recv()

    def build_kron(out, spread):
        step = size // 6

        def body(i, carry):
            at = pl.ds(pl.multiple_of(i * step, step), step)
            line = spread(level_of[at, :]).astype(BF16)
            full = dot(line, level_of[...], nt)
            same = dot(row_of[at, :], row_of[...], nt)
            out[at, :] = (full * same).astype(BF16)
            return carry

        lax.fori_loop(0, 6, body, 0)

    def vertical(kron, src, out):
        def body(i, carry):
            at = pl.ds(pl.multiple_of(i * chunk, chunk), chunk)
            out[at, :] = dot(kron[at, :], src[...]).astype(BF16)
            return carry

        lax.fori_loop(0, 3, body, 0)

    if n_lat == 2:
        sides = [(None, None)]
    else:
        sides = [(1, 1), (-1, 2)]

    def lat_copy(f, q):
        shift = sides[q][0]
        target = 1 - lat if shift is None else lat + shift
        return pltpu.make_async_remote_copy(
            src_ref=own_v.at[f], dst_ref=halo.at[f, q], send_sem=lat_s.at[f, q],
            recv_sem=lat_r.at[f, q],
            device_id={"lat": target}, device_id_type=MESH,
        )

    def sends(q):
        shift = sides[q][0]
        return None if shift is None else (lat < n_lat - 1 if shift == 1 else lat > 0)

    def receives(q):
        shift = sides[q][0]
        return None if shift is None else (lat > 0 if shift == 1 else lat < n_lat - 1)

    def under(condition, run):
        if condition is None:
            run()
        else:
            pl.when(condition)(run)

    def lat_send(f):
        for q in range(len(sides)):
            if sides[q][0] is not None:
                @pl.when(jnp.logical_not(receives(q)))
                def _():
                    halo[f, q] = jnp.zeros((size, cols), BF16)
            under(sends(q), lat_copy(f, q).start)

    def lat_finish(f):
        for q in range(len(sides)):
            under(receives(q), lat_copy(f, q).wait_recv)
        weights = []
        for q in range(len(sides)):
            if sides[q][0] is None:
                weights.append(jnp.where(lat == 1, lat_w[1], lat_w[2]))
            else:
                weights.append(lat_w[sides[q][1]])
        for g in range(levels // group):
            at = pl.ds(g * block, block)
            total = dot(lat_w[0], own_v[f, at, :])
            for q in range(len(sides)):
                total += dot(weights[q], halo[f, q, at, :])
            smoothed[f, at, :] = total.astype(BF16)

    def lon_copy(f, q):
        target = lax.rem(lon + (n_lon - 1 if q == 0 else 1), n_lon)
        return pltpu.make_async_remote_copy(
            src_ref=edge_out.at[f, q], dst_ref=edge_in.at[f, q], send_sem=lon_s.at[f, q],
            recv_sem=lon_r.at[f, q], device_id={"lon": target}, device_id_type=MESH,
        )

    def lon_send(f):
        for q in range(2):
            low = 0 if q == 0 else cols - LANES
            wide = jnp.concatenate(
                [smoothed[f, g * packed : (g + 1) * packed, low : low + LANES] for g in range(slots)],
                axis=1,
            )
            edge_out[f, q] = dot(wide, pack[q]).astype(BF16)
            lon_copy(f, q).start()

    def lon_finish(f, take):
        for q in range(2):
            lon_copy(f, q).wait_recv()
        for g in range(slots):
            at = pl.ds(g * packed, packed)
            mid = dot(smoothed[f, at, :], band[...])
            left = dot(edge_in[f, 1], halo_w[0, g])
            right = dot(edge_in[f, 0], halo_w[1, g])
            take(at, jnp.concatenate(
                [mid[:, :LANES] + left, mid[:, LANES:-LANES], mid[:, -LANES:] + right], axis=1
            ))

    inputs[0].wait()
    inputs[1].wait()
    build_kron(kron_c, lambda e: dot(e, mix[...]))
    inputs[2].wait()
    vertical(kron_c, control, own_v.at[0])
    lat_send(0)

    for p in range(away):
        arrived(mem, p)
        for d in range(1, members):
            for copy in leg_two(d, p):
                copy.start()

    build_kron(kron_f, lambda e: dot(e, mix[...], nt))
    for copy in inputs[3:]:
        copy.wait()
    lat_finish(0)
    lon_send(0)

    adjoint[...] = jnp.zeros((size, cols), F32)

    def scatter(blocks):
        for n, (val, cel) in enumerate(blocks):
            lanes = slice(n * half, (n + 1) * half)
            cell = cel.astype(F32)
            row = jnp.floor((cell + 0.5) * (1.0 / cols))
            col = cell - row * cols
            val32[...] = val.astype(F32)
            hit = lax.broadcasted_iota(jnp.int32, (rows, half), 0).astype(F32) == row

            def left(i, carry):
                two = [jnp.where(hit, val32[pl.ds(2 * i + k, 1), :], 0.0) for k in range(2)]
                at = pl.ds(pl.multiple_of(i * 2 * rows, 2 * rows), 2 * rows)
                lhs[at, lanes] = jnp.concatenate(two, axis=0).astype(BF16)
                return carry

            lax.fori_loop(0, levels // 2, left, 0)
            step = 64

            def right(i, carry):
                ids = (lax.broadcasted_iota(jnp.int32, (step, half), 0) + i * step).astype(F32)
                at = pl.ds(pl.multiple_of(i * step, step), step)
                rhs[at, lanes] = jnp.where(ids == col, 1.0, 0.0).astype(BF16)
                return carry

            lax.fori_loop(0, cols // step, right, 0)
        wide = len(blocks) * half

        def body(i, carry):
            at = pl.ds(pl.multiple_of(i * chunk, chunk), chunk)
            adjoint[at, :] += dot(lhs[at, :wide], rhs[:, :wide], nt)
            return carry

        lax.fori_loop(0, 3, body, 0)

    def near(d, carry):
        scatter([(loc_v[d, h], loc_c[d, h]) for h in range(parts)])
        return carry

    def far(owner):
        scatter([(got_v[owner, p], got_c[owner, p]) for p in range(away)])

    for copy in kept:
        copy.wait()
    for d in range(1, n_lat):
        for copy in straight(d):
            copy.wait_recv()
    lax.fori_loop(0, n_lat, near, 0)
    far(mem)

    def take_increment(at, smooth):
        inc32[at, :] = pert[at, :].astype(F32) * smooth

    lon_finish(0, take_increment)
    part = size // members

    def rs_copy(d):
        target = lax.rem(mem + d, members)
        return pltpu.make_async_remote_copy(
            src_ref=part_out.at[d], dst_ref=part_in.at[d], send_sem=rs_s.at[d],
            recv_sem=rs_r.at[d], device_id={"mem": target}, device_id_type=MESH,
        )

    for d in range(1, members):
        at = pl.ds(pl.multiple_of(lax.rem(mem + d, members) * part, part), part)
        part_out[d] = inc32[at, :].astype(BF16)
        rs_copy(d).start()

    def others(d, carry):
        owner = lax.rem(mem + members - d, members)
        for p in range(away):
            arrived(owner, p)
        far(owner)
        return carry

    lax.fori_loop(1, members - 1, others, 0)
    last = lax.rem(mem + 1, members)
    for p in range(away):
        arrived(last, p)
    far(last)

    field[...] = (pert[...].astype(F32) * adjoint[...]).astype(BF16)
    vertical(kron_f, field, own_v.at[1])
    lat_send(1)

    lat_finish(1)
    lon_send(1)
    total = inc32[pl.ds(pl.multiple_of(mem * part, part), part), :]
    for d in range(1, members):
        rs_copy(d).wait_recv()
        total += part_in[d].astype(F32)
    increment[...] = total

    lat_out[...] = smoothed[1]
    for q in range(2):
        lon_copy(1, q).wait_recv()
    edges[...] = edge_in[1]

    for o in range(1, n_lon):
        for copy in leg_one(o):
            copy.wait_send()
    for d in range(1, n_lat):
        for copy in straight(d):
            copy.wait_send()
    for p in range(away):
        for d in range(1, members):
            for copy in leg_two(d, p):
                copy.wait_send()
    for f in range(2):
        for q in range(len(sides)):
            under(sends(q), lat_copy(f, q).wait_send)
        for q in range(2):
            lon_copy(f, q).wait_send()
    for d in range(1, members):
        rs_copy(d).wait_send()


def last_kernel(control, smoothed, edges, band, halo_w, part, gradient, increment):
    def dot(a, b):
        return jnp.dot(a, b, preferred_element_type=F32)

    mid = dot(smoothed[...], band[...])
    left = dot(edges[1], halo_w[0, 0])
    right = dot(edges[0], halo_w[1, 0])
    own = control[...].astype(F32)
    gradient[:, :LANES] = own[:, :LANES] + (mid[:, :LANES] + left)
    gradient[:, LANES:-LANES] = own[:, LANES:-LANES] + mid[:, LANES:-LANES]
    gradient[:, -LANES:] = own[:, -LANES:] + (mid[:, -LANES:] + right)
    increment[...] = part[...]


def shards(sizes, control, ens_pert, vertical_mix, obs_values, obs_cells, obs_counts):
    members, n_lat, n_lon = sizes
    _, levels, rows, cols = control.shape
    tiles, cap = obs_values.shape[1], obs_values.shape[3]
    size = levels * rows
    parts = members // n_lat
    half = cap // parts
    away = n_lon - 1
    slots = LANES // 32
    packed = size // slots
    sides = 1 if n_lat == 2 else 2
    part = size // members
    dims = (levels, rows, cols, members, n_lat, n_lon, tiles, cap)
    dma = pltpu.SemaphoreType.DMA
    vmem = pl.BlockSpec(memory_space=pltpu.VMEM)
    hbm = pl.BlockSpec(memory_space=pl.ANY)
    group = group_of(levels, rows) * rows
    wide = max(parts, away) * half
    scratch = [
        pltpu.VMEM((size, cols), BF16),
        pltpu.VMEM((size, cols), BF16),
        pltpu.VMEM((size, levels), BF16),
        pltpu.VMEM((size, rows), BF16),
        pltpu.VMEM((3, group, group), BF16),
        pltpu.VMEM((cols, cols), BF16),
        pltpu.VMEM((2, slots * LANES, LANES), BF16),
        pltpu.VMEM((2, slots, LANES, LANES), BF16),
        pltpu.VMEM((tiles, parts, 1, half), jnp.int32),
        pltpu.VMEM((members, away, levels, half), BF16),
        pltpu.VMEM((members, away, 1, half), jnp.int32),
        pltpu.VMEM((n_lat, parts, levels, half), BF16),
        pltpu.VMEM((n_lat, parts, 1, half), jnp.int32),
        pltpu.VMEM((size, size), BF16),
        pltpu.VMEM((size, size), BF16),
        pltpu.VMEM((size, wide), BF16),
        pltpu.VMEM((cols, wide), BF16),
        pltpu.VMEM((levels, half), F32),
        pltpu.VMEM((size, cols), F32),
        pltpu.VMEM((size, cols), BF16),
        pltpu.VMEM((2, size, cols), BF16),
        pltpu.VMEM((2, sides, size, cols), BF16),
        pltpu.VMEM((2, size, cols), BF16),
        pltpu.VMEM((2, 2, packed, LANES), BF16),
        pltpu.VMEM((2, 2, packed, LANES), BF16),
        pltpu.VMEM((size, cols), F32),
        pltpu.VMEM((members, part, cols), BF16),
        pltpu.VMEM((members, part, cols), BF16),
        dma((8,)), dma((away, 2)), dma((members, away, 2)), dma((members, away, 2)),
        dma((n_lat, parts, 2)), dma((n_lat, parts, 2)),
        dma((2, sides)), dma((2, sides)), dma((2, 2)), dma((2, 2)),
        dma((members,)), dma((members,)),
    ]
    control = control.reshape(size, cols)
    level_of, row_of, lat_w, band, pack, halo_w = constants(levels, rows, cols)
    summed, smoothed, edges = pl.pallas_call(
        functools.partial(kernel, dims),
        out_shape=(
            jax.ShapeDtypeStruct((part, cols), F32),
            jax.ShapeDtypeStruct((size, cols), BF16),
            jax.ShapeDtypeStruct((2, packed, LANES), BF16),
        ),
        in_specs=[
            hbm, hbm, vmem, hbm, vmem, pl.BlockSpec(memory_space=pltpu.SMEM),
            hbm, hbm, hbm, hbm, hbm, hbm,
        ],
        out_specs=(vmem, vmem, vmem),
        scratch_shapes=scratch,
        compiler_params=pltpu.CompilerParams(
            collective_id=0, has_side_effects=True, vmem_limit_bytes=60 * 2**20
        ),
    )(
        control, ens_pert.reshape(size, cols), vertical_mix,
        obs_values.reshape(tiles, levels, cap), obs_cells.reshape(tiles, cap), obs_counts,
        level_of, row_of, lat_w, band, pack, halo_w,
    )
    rows_of = pl.BlockSpec((packed, cols), lambda g: (g, 0))
    if part % (8 * slots) == 0:
        part_of = pl.BlockSpec((part // slots, cols), lambda g: (g, 0))
    else:
        part_of = pl.BlockSpec((part, cols), lambda g: (0, 0))
    gradient, increment = pl.pallas_call(
        last_kernel,
        grid=(slots,),
        out_shape=(
            jax.ShapeDtypeStruct((size, cols), F32),
            jax.ShapeDtypeStruct((part, cols), F32),
        ),
        in_specs=[
            rows_of, rows_of,
            pl.BlockSpec((2, packed, LANES), lambda g: (0, 0, 0)),
            pl.BlockSpec((cols, cols), lambda g: (0, 0)),
            pl.BlockSpec((2, 1, LANES, LANES), lambda g: (0, g, 0, 0)),
            part_of,
        ],
        out_specs=(rows_of, part_of),
    )(control, smoothed, edges, band, halo_w, summed)
    return (
        increment.reshape(levels // members, rows, cols),
        gradient.reshape(1, levels, rows, cols),
    )


def solution(mesh):
    sizes = tuple(mesh.shape[a] for a in ("mem", "lat", "lon"))
    return jax.shard_map(
        functools.partial(shards, sizes),
        mesh=mesh,
        in_specs=(
            P("mem", None, "lat", "lon"),
            P("mem", None, "lat", "lon"),
            P(),
            P(("lat", "lon"), None, None, None),
            P(("lat", "lon"), None, None),
            P(("lat", "lon"), None),
        ),
        out_specs=(P("mem", "lat", "lon"), P("mem", None, "lat", "lon")),
        check_vma=False,
    )
```

profile of v0, /device:TPU:0, one launch (start us, length us, event | category | flops | bytes accessed | tf_op | source)
XLA Modules:
  0.0 56.0 jit_solution(7828370638946475442)
XLA Ops:
  0.6 50.4 %shard_map.131 = (f32[288,512]{1,0:T(8,128)}, bf16[1152,512]{1,0:T(8,128)(2,1)}, bf16[2,288,128]{2,1,0:T(8,128)(2,1)}) custom-call(bf16[1152,512]{1,0:T(8,128)(2,1)} %bitcast.6, bf16[1152,512]{1,0:T(8,128)(2,1)} %bitcast.8, bf16[48,48]{1,0:T(8,128)(2,1)} %mix.1, bf16[8,48,1024]{2,1,0:T(8,128)(2,1)} %bitcast.9, s32[8,1024]{1,0:T(8,128)} %bitcast.10, ...), custom_call_target="tpu_custom_call" | custom-call | tf_op jit(solution)/shard_map/pallas_call | solution.py:482
  51.0 4.9 %shard_map.132 = (f32[1152,512]{1,0:T(8,128)}, f32[288,512]{1,0:T(8,128)}) custom-call(bf16[1152,512]{1,0:T(8,128)(2,1)} %bitcast.7, bf16[1152,512]{1,0:T(8,128)(2,1)} %get-tuple-element.7.smoothed, bf16[2,288,128]{2,1,0:T(8,128)(2,1)} %get-tuple-element.8.edges, bf16[512,512]{1,0:T(8,128)(2,1)} %constant.15.clone.band_h.band, ...), custom_call_target="tpu_custom_call" | custom-call | tf_op jit(solution)/shard_map/pallas_call | solution.py:508
where the time goes:
time: 56.2 us; the launch traced here: 56 us
  Pallas kernels  55.3 us (98%)
  between operations  0.64 us (1%)
    pallas_call x1, Pallas kernels, shards(): pl.pallas_call(functools.partial(kernel, dims), out_shape=(jax.ShapeDtype...  50.4 us
    pallas_call x1, Pallas kernels, shards(): pl.pallas_call(last_kernel, grid=(slots,), out_shape=(jax.ShapeDtypeStruc...  4.91 us

commit v1 on v0

--- a/solution.py
+++ b/solution.py
@@ -11,6 +11,7 @@
 
 HALF = 24
 LANES = 128
+CHUNKS = 3
 MESH = pl.DeviceIdType.MESH
 F32 = jnp.float32
 BF16 = jnp.bfloat16
@@ -41,25 +42,27 @@
     band = taper_table((c[:, None] - c[None, :]).astype(np.float64))
     slots = LANES // 32
     pack = np.zeros((2, slots * LANES, LANES), np.float32)
-    halo_w = np.zeros((2, slots, LANES, LANES), np.float32)
+    halo_w = np.zeros((2, LANES, slots * LANES), np.float32)
     i = np.arange(LANES).astype(np.float64)
     for g in range(slots):
         for k in range(HALF):
             pack[0, g * LANES + k, 32 * g + k] = 1.0
             pack[1, g * LANES + LANES - HALF + k, 32 * g + k] = 1.0
-            halo_w[0, g, 32 * g + k] = taper_table(k - HALF - i)
-            halo_w[1, g, 32 * g + k] = taper_table(LANES + k - i)
+            at = slice(g * LANES, (g + 1) * LANES)
+            halo_w[0, 32 * g + k, at] = taper_table(k - HALF - i)
+            halo_w[1, 32 * g + k, at] = taper_table(LANES + k - i)
     return [jnp.asarray(a, BF16) for a in (level_of, row_of, lat_w, band, pack, halo_w)]
 
 
 def kernel(
     dims,
     control_h, pert_h, mix, values, cells, counts, level_h, row_h, lat_h, band_h, pack_h, halo_h,
-    increment, lat_out, edges,
+    increment_h, gradient_h,
     control, pert, level_of, row_of, lat_w, band, pack, halo_w,
-    live, got_v, got_c, loc_v, loc_c, kron_c, kron_f, lhs, rhs, val32, adjoint, field, own_v, halo,
-    smoothed, edge_out, edge_in, inc32, part_out, part_in,
-    in_s, s1, s2, r2, loc_s, loc_r, lat_s, lat_r, lon_s, lon_r, rs_s, rs_r,
+    live, got_v, got_c, loc_v, loc_c, kron_c, kron_f, lhs, rhs, val32, adjoint, field, field_l,
+    field_v, halo,
+    smoothed, edge_out, edge_in, inc32, part_out, part_in, total_out, grad,
+    in_s, s1, s2, r2, loc_s, loc_r, lat_s, lat_r, lon_s, lon_r, rs_s, rs_r, out_s,
 ):
     levels, rows, cols, members, n_lat, n_lon, tiles, cap = dims
     size = levels * rows
@@ -69,10 +72,10 @@
     mem, lat, lon = lax.axis_index("mem"), lax.axis_index("lat"), lax.axis_index("lon")
     tile = lat * n_lon + lon
     slots = LANES // 32
-    packed = size // slots
     group = group_of(levels, rows)
     block = group * rows
-    chunk = size // 3
+    chunk = size // CHUNKS
+    packed = chunk // slots
 
     def dot(a, b, dims=(((1,), (0,)), ((), ()))):
         return lax.dot_general(a, b, dims, preferred_element_type=F32)
@@ -185,25 +188,25 @@
 
         lax.fori_loop(0, 6, body, 0)
 
-    def vertical(kron, src, out):
-        def body(i, carry):
-            at = pl.ds(pl.multiple_of(i * chunk, chunk), chunk)
-            out[at, :] = dot(kron[at, :], src[...]).astype(BF16)
-            return carry
-
-        lax.fori_loop(0, 3, body, 0)
+    def vertical(kron, src, out, c):
+        at = pl.ds(c * chunk, chunk)
+        out[at, :] = dot(kron[at, :], src[...]).astype(BF16)
 
     if n_lat == 2:
         sides = [(None, None)]
     else:
         sides = [(1, 1), (-1, 2)]
 
-    def lat_copy(f, q):
+    def lat_copy(f, q, c):
         shift = sides[q][0]
         target = 1 - lat if shift is None else lat + shift
+        if f == 0:
+            src, dst = control_h, halo.at[0, q]
+        else:
+            at = pl.ds(c * chunk, chunk)
+            src, dst = field_v.at[at, :], halo.at[1, q, at, :]
         return pltpu.make_async_remote_copy(
-            src_ref=own_v.at[f], dst_ref=halo.at[f, q], send_sem=lat_s.at[f, q],
-            recv_sem=lat_r.at[f, q],
+            src_ref=src, dst_ref=dst, send_sem=lat_s.at[f, q, c], recv_sem=lat_r.at[f, q, c],
             device_id={"lat": target}, device_id_type=MESH,
         )
 
@@ -221,65 +224,86 @@
         else:
             pl.when(condition)(run)
 
-    def lat_send(f):
+    def lat_send(f, c):
+        for q in range(len(sides)):
+            under(sends(q), lat_copy(f, q, c).start)
+
+    def lat_clear(f):
         for q in range(len(sides)):
             if sides[q][0] is not None:
                 @pl.when(jnp.logical_not(receives(q)))
                 def _():
                     halo[f, q] = jnp.zeros((size, cols), BF16)
-            under(sends(q), lat_copy(f, q).start)
-
-    def lat_finish(f):
-        for q in range(len(sides)):
-            under(receives(q), lat_copy(f, q).wait_recv)
+
+    def lat_weights():
         weights = []
         for q in range(len(sides)):
             if sides[q][0] is None:
                 weights.append(jnp.where(lat == 1, lat_w[1], lat_w[2]))
             else:
                 weights.append(lat_w[sides[q][1]])
-        for g in range(levels // group):
+        return weights
+
+    def lat_arrived(f, c):
+        for q in range(len(sides)):
+            under(receives(q), lat_copy(f, q, c).wait_recv)
+
+    def lat_sum(f, src, out, weights, c):
+        for g in range(c * chunk // block, (c + 1) * chunk // block):
             at = pl.ds(g * block, block)
-            total = dot(lat_w[0], own_v[f, at, :])
+            total = dot(lat_w[0], src[at, :])
             for q in range(len(sides)):
                 total += dot(weights[q], halo[f, q, at, :])
-            smoothed[f, at, :] = total.astype(BF16)
-
-    def lon_copy(f, q):
+            out[at, :] = total.astype(BF16)
+
+    def lon_copy(f, q, c):
         target = lax.rem(lon + (n_lon - 1 if q == 0 else 1), n_lon)
         return pltpu.make_async_remote_copy(
-            src_ref=edge_out.at[f, q], dst_ref=edge_in.at[f, q], send_sem=lon_s.at[f, q],
-            recv_sem=lon_r.at[f, q], device_id={"lon": target}, device_id_type=MESH,
+            src_ref=edge_out.at[f, q, c], dst_ref=edge_in.at[f, q, c],
+            send_sem=lon_s.at[f, q, c], recv_sem=lon_r.at[f, q, c],
+            device_id={"lon": target}, device_id_type=MESH,
         )
 
-    def lon_send(f):
+    def lon_send(f, c):
         for q in range(2):
             low = 0 if q == 0 else cols - LANES
             wide = jnp.concatenate(
-                [smoothed[f, g * packed : (g + 1) * packed, low : low + LANES] for g in range(slots)],
+                [
+                    smoothed[f, c * chunk + g * packed : c * chunk + (g + 1) * packed, low : low + LANES]
+                    for g in range(slots)
+                ],
                 axis=1,
             )
-            edge_out[f, q] = dot(wide, pack[q]).astype(BF16)
-            lon_copy(f, q).start()
-
-    def lon_finish(f, take):
+            edge_out[f, q, c] = dot(wide, pack[q]).astype(BF16)
+            lon_copy(f, q, c).start()
+
+    def lon_sides(f, c):
         for q in range(2):
-            lon_copy(f, q).wait_recv()
-        for g in range(slots):
-            at = pl.ds(g * packed, packed)
-            mid = dot(smoothed[f, at, :], band[...])
-            left = dot(edge_in[f, 1], halo_w[0, g])
-            right = dot(edge_in[f, 0], halo_w[1, g])
-            take(at, jnp.concatenate(
-                [mid[:, :LANES] + left, mid[:, LANES:-LANES], mid[:, -LANES:] + right], axis=1
-            ))
-
+            lon_copy(f, q, c).wait_recv()
+
+        def rows_of(edge, weight):
+            flat = dot(edge, weight)
+            return jnp.concatenate(
+                [flat[:, g * LANES : (g + 1) * LANES] for g in range(slots)], axis=0
+            )
+
+        return rows_of(edge_in[f, 1, c], halo_w[0]), rows_of(edge_in[f, 0, c], halo_w[1])
+
+    lat_send(0, 0)
+    lat_clear(0)
+    lat_clear(1)
     inputs[0].wait()
     inputs[1].wait()
     build_kron(kron_c, lambda e: dot(e, mix[...]))
-    inputs[2].wait()
-    vertical(kron_c, control, own_v.at[0])
-    lat_send(0)
+    for copy in inputs[2:]:
+        copy.wait()
+    weights = lat_weights()
+    lat_arrived(0, 0)
+    for c in range(CHUNKS):
+        lat_sum(0, control, field_l, weights, c)
+    for c in range(CHUNKS):
+        vertical(kron_c, field_l, smoothed.at[0], c)
+        lon_send(0, c)
 
     for p in range(away):
         arrived(mem, p)
@@ -288,10 +312,6 @@
                 copy.start()
 
     build_kron(kron_f, lambda e: dot(e, mix[...], nt))
-    for copy in inputs[3:]:
-        copy.wait()
-    lat_finish(0)
-    lon_send(0)
 
     adjoint[...] = jnp.zeros((size, cols), F32)
 
@@ -342,12 +362,15 @@
         for copy in straight(d):
             copy.wait_recv()
     lax.fori_loop(0, n_lat, near, 0)
-    far(mem)
-
-    def take_increment(at, smooth):
+
+    for c in range(CHUNKS):
+        at = pl.ds(c * chunk, chunk)
+        mid = dot(smoothed[0, at, :], band[...])
+        left, right = lon_sides(0, c)
+        smooth = jnp.concatenate(
+            [mid[:, :LANES] + left, mid[:, LANES:-LANES], mid[:, -LANES:] + right], axis=1
+        )
         inc32[at, :] = pert[at, :].astype(F32) * smooth
-
-    lon_finish(0, take_increment)
     part = size // members
 
     def rs_copy(d):
@@ -362,6 +385,8 @@
         part_out[d] = inc32[at, :].astype(BF16)
         rs_copy(d).start()
 
+    far(mem)
+
     def others(d, carry):
         owner = lax.rem(mem + members - d, members)
         for p in range(away):
@@ -376,21 +401,33 @@
     far(last)
 
     field[...] = (pert[...].astype(F32) * adjoint[...]).astype(BF16)
-    vertical(kron_f, field, own_v.at[1])
-    lat_send(1)
-
-    lat_finish(1)
-    lon_send(1)
+    for c in range(CHUNKS):
+        vertical(kron_f, field, field_v, c)
+        lat_send(1, c)
+    for c in range(CHUNKS):
+        lat_arrived(1, c)
+        lat_sum(1, field_v, smoothed.at[1], weights, c)
+        lon_send(1, c)
+    for c in range(CHUNKS):
+        at = pl.ds(c * chunk, chunk)
+        grad[at, :] = control[at, :].astype(F32) + dot(smoothed[1, at, :], band[...])
+
     total = inc32[pl.ds(pl.multiple_of(mem * part, part), part), :]
     for d in range(1, members):
         rs_copy(d).wait_recv()
         total += part_in[d].astype(F32)
-    increment[...] = total
-
-    lat_out[...] = smoothed[1]
-    for q in range(2):
-        lon_copy(1, q).wait_recv()
-    edges[...] = edge_in[1]
+    total_out[...] = total
+    outputs = [pltpu.make_async_copy(total_out, increment_h, out_s.at[CHUNKS])]
+    outputs[0].start()
+    for c in range(CHUNKS):
+        at = pl.ds(c * chunk, chunk)
+        left, right = lon_sides(1, c)
+        grad[at, :LANES] += left
+        grad[at, cols - LANES :] += right
+        outputs.append(pltpu.make_async_copy(grad.at[at, :], gradient_h.at[at, :], out_s.at[c]))
+        outputs[-1].start()
+    for copy in outputs:
+        copy.wait()
 
     for o in range(1, n_lon):
         for copy in leg_one(o):
@@ -402,27 +439,16 @@
         for d in range(1, members):
             for copy in leg_two(d, p):
                 copy.wait_send()
+    for q in range(len(sides)):
+        under(sends(q), lat_copy(0, q, 0).wait_send)
+        for c in range(CHUNKS):
+            under(sends(q), lat_copy(1, q, c).wait_send)
     for f in range(2):
-        for q in range(len(sides)):
-            under(sends(q), lat_copy(f, q).wait_send)
         for q in range(2):
-            lon_copy(f, q).wait_send()
+            for c in range(CHUNKS):
+                lon_copy(f, q, c).wait_send()
     for d in range(1, members):
         rs_copy(d).wait_send()
-
-
-def last_kernel(control, smoothed, edges, band, halo_w, part, gradient, increment):
-    def dot(a, b):
-        return jnp.dot(a, b, preferred_element_type=F32)
-
-    mid = dot(smoothed[...], band[...])
-    left = dot(edges[1], halo_w[0, 0])
-    right = dot(edges[0], halo_w[1, 0])
-    own = control[...].astype(F32)
-    gradient[:, :LANES] = own[:, :LANES] + (mid[:, :LANES] + left)
-    gradient[:, LANES:-LANES] = own[:, LANES:-LANES] + mid[:, LANES:-LANES]
-    gradient[:, -LANES:] = own[:, -LANES:] + (mid[:, -LANES:] + right)
-    increment[...] = part[...]
 
 
 def shards(sizes, control, ens_pert, vertical_mix, obs_values, obs_cells, obs_counts):
@@ -434,7 +460,7 @@
     half = cap // parts
     away = n_lon - 1
     slots = LANES // 32
-    packed = size // slots
+    packed = size // CHUNKS // slots
     sides = 1 if n_lat == 2 else 2
     part = size // members
     dims = (levels, rows, cols, members, n_lat, n_lon, tiles, cap)
@@ -451,7 +477,7 @@
         pltpu.VMEM((3, group, group), BF16),
         pltpu.VMEM((cols, cols), BF16),
         pltpu.VMEM((2, slots * LANES, LANES), BF16),
-        pltpu.VMEM((2, slots, LANES, LANES), BF16),
+        pltpu.VMEM((2, LANES, slots * LANES), BF16),
         pltpu.VMEM((tiles, parts, 1, half), jnp.int32),
         pltpu.VMEM((members, away, levels, half), BF16),
         pltpu.VMEM((members, away, 1, half), jnp.int32),
@@ -464,33 +490,35 @@
         pltpu.VMEM((levels, half), F32),
         pltpu.VMEM((size, cols), F32),
         pltpu.VMEM((size, cols), BF16),
-        pltpu.VMEM((2, size, cols), BF16),
+        pltpu.VMEM((size, cols), BF16),
+        pltpu.VMEM((size, cols), BF16),
         pltpu.VMEM((2, sides, size, cols), BF16),
         pltpu.VMEM((2, size, cols), BF16),
-        pltpu.VMEM((2, 2, packed, LANES), BF16),
-        pltpu.VMEM((2, 2, packed, LANES), BF16),
+        pltpu.VMEM((2, 2, CHUNKS, packed, LANES), BF16),
+        pltpu.VMEM((2, 2, CHUNKS, packed, LANES), BF16),
         pltpu.VMEM((size, cols), F32),
         pltpu.VMEM((members, part, cols), BF16),
         pltpu.VMEM((members, part, cols), BF16),
+        pltpu.VMEM((part, cols), F32),
+        pltpu.VMEM((size, cols), F32),
         dma((8,)), dma((away, 2)), dma((members, away, 2)), dma((members, away, 2)),
         dma((n_lat, parts, 2)), dma((n_lat, parts, 2)),
-        dma((2, sides)), dma((2, sides)), dma((2, 2)), dma((2, 2)),
-        dma((members,)), dma((members,)),
+        dma((2, sides, CHUNKS)), dma((2, sides, CHUNKS)), dma((2, 2, CHUNKS)), dma((2, 2, CHUNKS)),
+        dma((members,)), dma((members,)), dma((CHUNKS + 1,)),
     ]
     control = control.reshape(size, cols)
     level_of, row_of, lat_w, band, pack, halo_w = constants(levels, rows, cols)
-    summed, smoothed, edges = pl.pallas_call(
+    increment, gradient = pl.pallas_call(
         functools.partial(kernel, dims),
         out_shape=(
             jax.ShapeDtypeStruct((part, cols), F32),
-            jax.ShapeDtypeStruct((size, cols), BF16),
-            jax.ShapeDtypeStruct((2, packed, LANES), BF16),
+            jax.ShapeDtypeStruct((size, cols), F32),
         ),
         in_specs=[
             hbm, hbm, vmem, hbm, vmem, pl.BlockSpec(memory_space=pltpu.SMEM),
             hbm, hbm, hbm, hbm, hbm, hbm,
         ],
-        out_specs=(vmem, vmem, vmem),
+        out_specs=(hbm, hbm),
         scratch_shapes=scratch,
         compiler_params=pltpu.CompilerParams(
             collective_id=0, has_side_effects=True, vmem_limit_bytes=60 * 2**20
@@ -500,27 +528,6 @@
         obs_values.reshape(tiles, levels, cap), obs_cells.reshape(tiles, cap), obs_counts,
         level_of, row_of, lat_w, band, pack, halo_w,
     )
-    rows_of = pl.BlockSpec((packed, cols), lambda g: (g, 0))
-    if part % (8 * slots) == 0:
-        part_of = pl.BlockSpec((part // slots, cols), lambda g: (g, 0))
-    else:
-        part_of = pl.BlockSpec((part, cols), lambda g: (0, 0))
-    gradient, increment = pl.pallas_call(
-        last_kernel,
-        grid=(slots,),
-        out_shape=(
-            jax.ShapeDtypeStruct((size, cols), F32),
-            jax.ShapeDtypeStruct((part, cols), F32),
-        ),
-        in_specs=[
-            rows_of, rows_of,
-            pl.BlockSpec((2, packed, LANES), lambda g: (0, 0, 0)),
-            pl.BlockSpec((cols, cols), lambda g: (0, 0)),
-            pl.BlockSpec((2, 1, LANES, LANES), lambda g: (0, g, 0, 0)),
-            part_of,
-        ],
-        out_specs=(rows_of, part_of),
-    )(control, smoothed, edges, band, halo_w, summed)
     return (
         increment.reshape(levels // members, rows, cols),
         gradient.reshape(1, levels, rows, cols),

time: 56.2 us -> 55 us (0.979)
  Pallas kernels: 55.3 us -> 48.9 us
  local copies, waits for them, and re-layouts: 0 us -> 5.2 us
    unnamed x0 -> x2, local copies, waits for them, and re-layouts: none -> 5.2 us
    pallas_call x1 -> x0, Pallas kernels: 4.91 us -> none  [shards(): pl.pallas_call(last_kernel, grid=(slots,), out_shape=(jax.ShapeDtypeStruc...]
    pallas_call x1, Pallas kernels: 50.4 us -> 48.9 us  [shards(): pl.pallas_call(functools.partial(kernel, dims), out_shape=(jax.ShapeDtype...]
where the time goes in v1:
time: 55 us; the launch traced here: 54.8 us
  Pallas kernels  48.9 us (89%)
  local copies, waits for them, and re-layouts  5.2 us (9%)
  between operations  0.64 us (1%)
    pallas_call x1, Pallas kernels, shards(): pl.pallas_call(functools.partial(kernel, dims), out_shape=(jax.ShapeDtype...  48.9 us
    unnamed x2, local copies, waits for them, and re-layouts  5.2 us

profile of v1, /device:TPU:0, one launch (start us, length us, event | category | flops | bytes accessed | tf_op | source)
XLA Modules:
  0.0 54.8 jit_solution(11117011297817170346)
XLA Ops:
  0.6 48.9 %shard_map.131 = (f32[288,512]{1,0:T(8,128)}, f32[1152,512]{1,0:T(8,128)}) custom-call(bf16[1152,512]{1,0:T(8,128)(2,1)} %bitcast.7, bf16[1152,512]{1,0:T(8,128)(2,1)} %bitcast.8, bf16[48,48]{1,0:T(8,128)(2,1)} %mix.1, bf16[8,48,1024]{2,1,0:T(8,128)(2,1)} %bitcast.9, s32[8,1024]{1,0:T(8,128)} %bitcast.11, s32[1,8]{1,0:T(1,128)} %counts.1, ...), custom_call_target="tpu_custom_call" | custom-call | tf_op jit(solution)/shard_map/pallas_call | solution.py:511
  49.6 1.9 %copy.16 = f32[12,24,512]{2,1,0:T(8,128)} copy(f32[12,24,512]{2,1,0:T(8,128)} %bitcast.10) | data formatting | bytes 1179648
  51.5 3.3 %copy.17 = f32[1,48,24,512]{3,2,1,0:T(8,128)} copy(f32[1,48,24,512]{3,2,1,0:T(8,128)} %bitcast.6) | data formatting | bytes 4718592
